TPU v7x, 32 devices: a whole 2x2x4 slice. The times are simulated.
32 devices in a mesh: band: 4 (over x, core), row: 8 (over z, y).
Axes of the slice: x: 2, y: 2, z: 4, core: 2. Of those that a mesh axis runs over, the one named last changes fastest.
Arguments:
- shape_coupling_matrices: bfloat16 [512, 4, 128, 128], P('row'), may hold values from 0 to 0.00390625
- target_strip_index: int32 [512, 4], P('row'), may hold values from 0 to 511, as said below
- occupied_entries_per_strip: int32 [512], P('row'), may hold values from 1 to 4
- prior_leaving_energy: bfloat16 [4, 65536], P('band', 'row'), may hold values from 0.19921875 to 3
- facet_kelvins: float32 [65536], P('row'), may hold values from 0.6 to 1.6
- emitting_ability: float32 [4, 65536], P('band', 'row'), may hold values from 0.2 to 0.9
- centre_frequency: float32 [4], P('band'), may hold values from 0.28 to 6.3
- frequency_span: float32 [4], P('band'), may hold values from 0.5 to 1.5
- prescribed_power_density: float32 [65536], P('row'), may hold values from -6 to 6
Outputs:
- corrected_kelvins: float32 [65536], P('row')
- refreshed_leaving_energy: float32 [4, 65536], P('band', 'row')
Inputs may be any that keep to these rules, and one draw needn't show every extreme that they name: `target_strip_index`: of the 256 entries of one device's rows, exactly 32 name a column tile held by each index of row.
All inputs are finite; a program needn't handle non-finite values.
Results may differ from a plain program's by a relative error of at most 0.0003.
Values may be sent and summed in bfloat16 or wider, within the bound.
No kernel may reach another device: no remote copies, remote signals or barrier semaphores. Data moves between devices by JAX's collectives and lax.ppermute only.
A program may use at most 64 MiB of HBM per device.

v0:
```python
import jax
import jax.numpy as jnp
from jax import lax
from jax.sharding import PartitionSpec as P


def emitter_terms(centre_sample, frequency_spacing, facet_kelvins):
    return (
        frequency_spacing[:, None]
        * centre_sample[:, None] ** 3
        / jnp.expm1(centre_sample[:, None] / facet_kelvins[None, :])
    )


def on_device(
    shape_coupling_matrices,
    target_strip_index,
    occupied_entries_per_strip,
    prior_leaving_energy,
    facet_kelvins,
    emitting_ability,
    centre_frequency,
    frequency_span,
    prescribed_power_density,
):
    bands_here, facets_here = prior_leaving_energy.shape
    tile_rows, slot_count = target_strip_index.shape
    tile_size = shape_coupling_matrices.shape[2]
    entries = tile_rows * slot_count
    flat_cols = target_strip_index.reshape(entries)
    gathered = lax.all_gather(prior_leaving_energy, "row", axis=1, tiled=True)
    picked = gathered.reshape(bands_here, -1, tile_size)[:, flat_cols]
    picked = picked.reshape(bands_here, tile_rows, slot_count, tile_size)
    slot_used = (
        lax.broadcasted_iota(jnp.int32, (tile_rows, slot_count), 1)
        < occupied_entries_per_strip[:, None]
    )
    masked = jnp.where(slot_used[None, :, :, None], picked, jnp.zeros_like(picked))
    incoming = jnp.einsum(
        "rkij,brkj->bri", shape_coupling_matrices, masked, preferred_element_type=jnp.float32
    ).reshape(bands_here, facets_here)
    partial_terms = emitter_terms(centre_frequency, frequency_span, facet_kelvins)
    planck_sum = lax.psum(jnp.sum(partial_terms, 0), "band")
    energy_portion = partial_terms / planck_sum
    kelvins_third_power = facet_kelvins**3
    ideal_emitter_power = energy_portion * kelvins_third_power * facet_kelvins
    refreshed_leaving_energy = (
        emitting_ability * ideal_emitter_power + (1.0 - emitting_ability) * incoming
    )
    quotient = emitting_ability / (1.0 - emitting_ability)
    flux_part = jnp.sum(quotient * (ideal_emitter_power - refreshed_leaving_energy), 0)
    gradient_piece = jnp.sum(quotient * 4.0 * energy_portion * kelvins_third_power, 0)
    balance_power_density, power_gradient = lax.psum((flux_part, gradient_piece), "band")
    corrected_kelvins = (
        facet_kelvins - (balance_power_density - prescribed_power_density) / power_gradient
    )
    return (corrected_kelvins, refreshed_leaving_energy)


def solution(mesh):
    in_specs = (
        P("row", None, None, None),
        P("row", None),
        P("row"),
        P("band", "row"),
        P("row"),
        P("band", "row"),
        P("band"),
        P("band"),
        P("row"),
    )
    out_specs = (P("row"), P("band", "row"))
    return jax.shard_map(
        on_device, mesh=mesh, in_specs=in_specs, out_specs=out_specs, check_vma=False
    )
```

profile of v0, /device:TPU:0, one launch (start us, length us, event | category | flops | bytes accessed | tf_op | source)
XLA Modules:
  0.0 104.3 jit_solution(12224050853336227778)
XLA Ops:
  7.2 0.0 copy-start
  7.2 0.0 copy-start.1
  7.2 0.0 all-reduce.3.cloned.1.call-start
  8.5 0.8 broadcast_divide_fusion
  9.3 12.9 %psum.21 = f32[8192]{0:T(1024)S(1)} all-reduce(f32[8192]{0:T(1024)S(1)} %broadcast_divide_fusion), channel_id=1, replica_groups=mesh['band'=4,'row'=8] {'band'}, use_global_device_ids=true, to_apply=%region_0.1 | all-reduce | flops 8192 | bytes 65536 | tf_op jit(solution)/shard_map/psum | solution.py:43
  22.2 31.3 %all_gather.3 = bf16[1,65536]{1,0:T(2,128)(2,1)S(1)} all-gather(bf16[1,8192]{1,0:T(2,128)(2,1)} %param.12), channel_id=1, replica_groups=mesh['band'=4,'row'=8] {'row'}, dimensions={1}, use_global_device_ids=true | all-gather | bytes 147456 | tf_op jit(solution)/shard_map/all_gather | solution.py:31
  53.5 0.8 copy.11
  54.3 0.1 reshape.85
  54.4 0.7 iota_compare_fusion
  55.1 0.8 multiply_multiply_fusion.2
  55.9 0.8 reduce
  56.7 0.9 gather_fusion
  57.6 0.1 select_bitcast_fusion
  57.7 6.3 %subtract_multiply_fusion = (f32[1,8192]{1,0:T(1,128)}, f32[1,8192]{1,0:T(1,128)S(1)}, f32[1,8192]{1,0:T(1,128)}) fusion(f32[1,8192]{1,0:T(1,128)S(1)} %bitcast.36, f32[1,8192]{1,0:T(1,128)} %param.14, bf16[64,4,128,128]{3,2,1,0:T(8,128)(2,1)} %param.9, bf16[64,4,128,1]{2,1,0,3:T(4,128)(2,1)S(1)} %select_bitcast_fusion), kind=kOutput, calls=%fused_computation.10 | convolution fusion | flops 8445952 | bytes 8617984 | tf_op jit(solution)/shard_map/rkij,brkj->bri/dot_general | solution.py:39
  64.0 0.7 multiply_multiply_fusion.1
  64.7 0.0 all-reduce.3.cloned.1.call-update
  64.7 31.3 %all-reduce.3.cloned.1.call-done = (f32[8192]{0:T(1024)}, f32[8192]{0:T(1024)}) async-done(((f32[8192]{0:T(1024)}, f32[8192]{0:T(1024)}), (f32[8192]{0:T(1024)}, f32[8192]{0:T(1024)})) %all-reduce.3.cloned.1.call-update) | async-done | bytes 65552 | tf_op jit(solution)/shard_map/psum | solution.py:53
  96.0 0.0 copy-done
  96.0 0.0 copy-done.1
  96.0 1.4 %divide_subtract_fusion = f32[8192]{0:T(1024)} fusion(f32[8192]{0:T(1024)S(1)} %copy-done, f32[8192]{0:T(1024)} %get-tuple-element.2, f32[8192]{0:T(1024)} %get-tuple-element.3, f32[8192]{0:T(1024)S(1)} %copy-done.1), kind=kLoop, calls=%fused_computation.8 | loop fusion | flops 24576 | bytes 163840 | tf_op jit(solution)/shard_map/sub | solution.py:55
  (2 shorter events, 0.0 us)
Async XLA Ops:
  7.2 88.8 %copy-start = (f32[8192]{0:T(1024)S(1)}, f32[8192]{0:T(1024)}, u32[]{:S(2)}) copy-start(f32[8192]{0:T(1024)} %param.13) | copy-start | bytes 98308
  7.2 88.8 %copy-start.1 = (f32[8192]{0:T(1024)S(1)}, f32[8192]{0:T(1024)}, u32[]{:S(2)}) copy-start(f32[8192]{0:T(1024)} %param.17) | copy-start | bytes 98308
  7.2 88.8 %all-reduce.3.cloned.1.call-start = ((), (), s32[]{:S(2)}) async-start(), calls=%async_computation | async-start | bytes 131072 | tf_op jit(solution)/shard_map/psum | solution.py:53
Sparse Core Ops, SparseCore 0:
  64.8 31.1 all-reduce.2
where the time goes:
time: 105 us; the launch traced here: 104 us
  blocking collectives  44.2 us (42%)
  waiting for transfers between devices  31.3 us (30%)
  between operations  15.4 us (15%)
  matrix products  6.3 us (6%)
  other arithmetic  5.3 us (5%)
  local copies, waits for them, and re-layouts  1.74 us (2%)
    psum x1, waiting for transfers between devices, on_device(): lax.psum((flux_part, gradient_piece), 'band')  31.3 us
    all_gather x1, blocking collectives, on_device(): gathered = lax.all_gather(prior_leaving_energy, 'row', axis=1, tiled=True)  31.3 us
    psum x1, blocking collectives, on_device(): planck_sum = lax.psum(jnp.sum(partial_terms, 0), 'band')  12.9 us
    dot_general x1, matrix products, on_device(): jnp.einsum('rkij,brkj->bri', shape_coupling_matrices, masked, preferred_e...  6.3 us
  transfers between devices with their start and end apart: 1, of which 1 were waited for; matrix products, arithmetic and copies ran while one was open for 0% of the time, Pallas kernels for 0%

commit v1 on v0

--- a/solution.py
+++ b/solution.py
@@ -2,6 +2,28 @@
 import jax.numpy as jnp
 from jax import lax
 from jax.sharding import PartitionSpec as P
+
+
+def laid_out(tiles, dim):
+    tiles = jnp.moveaxis(tiles, 0, dim)
+    shape = tiles.shape
+    return tiles.reshape(*shape[:dim], shape[dim] * shape[dim + 1], *shape[dim + 2 :])
+
+
+def collected_by_bits(x, axis):
+    peers = lax.axis_size(axis)
+    blocks = x[None]
+    for level in range(peers.bit_length() - 1):
+        stride = 1 << level
+        other = lax.ppermute(blocks, axis, [(i, i ^ stride) for i in range(peers)])
+        both = jnp.stack([blocks, other])
+        upper = lax.axis_index(axis) >> level & 1
+        blocks = jnp.where(upper == 0, both, both[::-1]).reshape(-1, *x.shape)
+    return blocks
+
+
+def doubled_up(value, axis, dim):
+    return laid_out(collected_by_bits(value, axis), dim)
 
 
 def emitter_terms(centre_sample, frequency_spacing, facet_kelvins):
@@ -28,7 +50,7 @@
     tile_size = shape_coupling_matrices.shape[2]
     entries = tile_rows * slot_count
     flat_cols = target_strip_index.reshape(entries)
-    gathered = lax.all_gather(prior_leaving_energy, "row", axis=1, tiled=True)
+    gathered = doubled_up(prior_leaving_energy, "row", 1)
     picked = gathered.reshape(bands_here, -1, tile_size)[:, flat_cols]
     picked = picked.reshape(bands_here, tile_rows, slot_count, tile_size)
     slot_used = (

time: 105 us -> 87.2 us (0.83)
  blocking collectives: 44.2 us -> 10.8 us
  starting transfers between devices: 0.04 us -> 7.37 us
  waiting for transfers between devices: 31.3 us -> 36.7 us
  local copies, waits for them, and re-layouts: 1.74 us -> 3.61 us
  other arithmetic: 5.3 us -> 6.52 us
    all_gather x1 -> x0, blocking collectives: 31.3 us -> none  [on_device(): gathered = lax.all_gather(prior_leaving_energy, 'row', axis=1, tiled=True)]
    ppermute x0 -> x3, starting transfers between devices: none -> 7.33 us  [collected_by_bits(): other = lax.ppermute(blocks, axis, [(i, i ^ stride) for i in range(peers)])]
    ppermute x0 -> x3, waiting for transfers between devices: none -> 4.88 us  [collected_by_bits(): other = lax.ppermute(blocks, axis, [(i, i ^ stride) for i in range(peers)])]
    psum x1, blocking collectives: 12.9 us -> 10.8 us  [on_device(): planck_sum = lax.psum(jnp.sum(partial_terms, 0), 'band')]
    another operation x0 -> x4, other arithmetic: none -> 1.88 us  [collected_by_bits(): both = jnp.stack([blocks, other])]
    rev x0 -> x1, local copies, waits for them, and re-layouts: none -> 1.65 us  [collected_by_bits(): blocks = jnp.where(upper == 0, both, both[::-1]).reshape(-1, *x.shape)]
  transfers between devices with their start and end apart: 1 -> 4, of which waited for: 1 -> 3; matrix products, arithmetic and copies ran while one was open for 0% -> 4% of each run, Pallas kernels for 0% -> 0%
where the time goes in v1:
time: 87.2 us; the launch traced here: 86.7 us
  waiting for transfers between devices  36.7 us (42%)
  between operations  15.4 us (18%)
  blocking collectives  10.8 us (12%)
  starting transfers between devices  7.37 us (8%)
  other arithmetic  6.52 us (7%)
  matrix products  6.3 us (7%)
  local copies, waits for them, and re-layouts  3.61 us (4%)
    psum x1, waiting for transfers between devices, on_device(): lax.psum((flux_part, gradient_piece), 'band')  31.8 us
    psum x1, blocking collectives, on_device(): planck_sum = lax.psum(jnp.sum(partial_terms, 0), 'band')  10.8 us
    ppermute x3, starting transfers between devices, collected_by_bits(): other = lax.ppermute(blocks, axis, [(i, i ^ stride) for i in range(peers)])  7.33 us
    dot_general x1, matrix products, on_device(): jnp.einsum('rkij,brkj->bri', shape_coupling_matrices, masked, preferred_e...  6.3 us
    ppermute x3, waiting for transfers between devices, collected_by_bits(): other = lax.ppermute(blocks, axis, [(i, i ^ stride) for i in range(peers)])  4.88 us
    another operation x4, other arithmetic, collected_by_bits(): both = jnp.stack([blocks, other])  1.88 us
  transfers between devices with their start and end apart: 4, of which 3 were waited for; matrix products, arithmetic and copies ran while one was open for 4% of the time, Pallas kernels for 0%

profile of v1, /device:TPU:0, one launch (start us, length us, event | category | flops | bytes accessed | tf_op | source)
XLA Modules:
  0.0 86.7 jit_solution(5238730422590684484)
XLA Ops:
  7.2 0.0 copy-start
  7.2 0.0 copy-start.1
  7.2 0.0 all-reduce.3.cloned.1.call-start
  7.2 3.0 %collective-permute-start = (bf16[1,1,8192]{2,1,0:T(2,128)(2,1)}, bf16[1,1,8192]{2,1,0:T(2,128)(2,1)S(1)}, u32[]{:S(2)}, u32[]{:S(2)}) collective-permute-start(bf16[1,1,8192]{2,1,0:T(2,128)(2,1)} %bitcast.48), channel_id=1, source_target_pairs={{0,1},{1,0},{2,3},{3,2},{4,5},{5,4},{6,7},{7,6},{8,9},{9,8},{10,11... | collective-permute-start | bytes 49160 | tf_op jit(solution)/shard_map/ppermute | solution.py:18
  11.6 0.8 broadcast_divide_fusion
  12.4 10.8 %psum.21 = f32[8192]{0:T(1024)S(1)} all-reduce(f32[8192]{0:T(1024)S(1)} %broadcast_divide_fusion), channel_id=1, replica_groups=mesh['band'=4,'row'=8] {'band'}, use_global_device_ids=true, to_apply=%region_0.1 | all-reduce | flops 8192 | bytes 65536 | tf_op jit(solution)/shard_map/psum | solution.py:65
  23.2 0.8 multiply_multiply_fusion.2
  24.0 0.7 iota_compare_fusion
  24.7 0.8 copy.13
  25.5 0.1 reshape.89
  25.6 0.0 collective-permute-done
  25.6 0.8 pad_maximum_fusion.2
  26.4 1.7 %rev.9 = bf16[2,1,1,8192]{3,0,2,1:T(2,128)(2,1)S(1)} reverse(bf16[2,1,1,8192]{3,0,2,1:T(2,128)(2,1)S(1)} %pad_maximum_fusion.2), dimensions={0} | reverse | bytes 65536 | tf_op jit(solution)/shard_map/rev | solution.py:21
  28.1 0.9 fusion.4
  29.0 1.6 %collective-permute-start.1 = (bf16[2,1,8192]{2,0,1:T(2,128)(2,1)S(1)}, bf16[2,1,8192]{2,0,1:T(2,128)(2,1)S(1)}, u32[]{:S(2)}, u32[]{:S(2)}) collective-permute-start(bf16[2,1,8192]{2,0,1:T(2,128)(2,1)S(1)} %get-tuple-element.9), channel_id=1, source_target_pairs={{0,2},{1,3},{2,0},{3,1},{4,6},{5,7},{6,4},{7,5},{8,10},{9,11},{10,... | collective-permute-start | bytes 98312 | tf_op jit(solution)/shard_map/ppermute | solution.py:18
  30.6 2.3 %collective-permute-done.1 = bf16[2,1,8192]{2,0,1:T(2,128)(2,1)S(1)} collective-permute-done((bf16[2,1,8192]{2,0,1:T(2,128)(2,1)S(1)}, bf16[2,1,8192]{2,0,1:T(2,128)(2,1)S(1)}, u32[]{:S(2)}, u32[]{:S(2)}) %collective-permute-start.1) | collective-permute-done | bytes 32800 | tf_op jit(solution)/shard_map/ppermute | solution.py:18
  32.9 0.1 pad_maximum_fusion.1
  33.0 0.1 broadcast_select_fusion
  33.1 2.7 %collective-permute-start.2 = (bf16[4,1,8192]{2,0,1:T(4,128)(2,1)S(1)}, bf16[4,1,8192]{2,0,1:T(4,128)(2,1)S(1)}, u32[]{:S(2)}, u32[]{:S(2)}) collective-permute-start(bf16[4,1,8192]{2,0,1:T(4,128)(2,1)S(1)} %reshape.88), channel_id=1, source_target_pairs={{0,4},{1,5},{2,6},{3,7},{4,0},{5,1},{6,2},{7,3},{8,12},{9,13},{10,... | collective-permute-start | bytes 196616 | tf_op jit(solution)/shard_map/ppermute | solution.py:18
  35.8 2.5 %collective-permute-done.2 = bf16[4,1,8192]{2,0,1:T(4,128)(2,1)S(1)} collective-permute-done((bf16[4,1,8192]{2,0,1:T(4,128)(2,1)S(1)}, bf16[4,1,8192]{2,0,1:T(4,128)(2,1)S(1)}, u32[]{:S(2)}, u32[]{:S(2)}) %collective-permute-start.2) | collective-permute-done | bytes 65568 | tf_op jit(solution)/shard_map/ppermute | solution.py:18
  38.4 0.1 pad_maximum_fusion
  38.5 0.1 reverse_select_fusion
  38.5 0.2 reshape.91
  38.7 0.9 gather_fusion
  39.6 0.1 select_bitcast_fusion
  39.7 6.3 %subtract_multiply_fusion = (f32[1,8192]{1,0:T(1,128)}, f32[1,8192]{1,0:T(1,128)S(1)}, f32[1,8192]{1,0:T(1,128)}) fusion(f32[1,8192]{1,0:T(1,128)S(1)} %bitcast.57, f32[1,8192]{1,0:T(1,128)} %param.14, bf16[64,4,128,128]{3,2,1,0:T(8,128)(2,1)} %param.9, bf16[64,4,128,1]{2,1,0,3:T(4,128)(2,1)S(1)} %select_bitcast_fusion), kind=kOutput, calls=%fused_computation.16 | convolution fusion | flops 8445952 | bytes 8617984 | tf_op jit(solution)/shard_map/rkij,brkj->bri/dot_general | solution.py:61
  46.0 0.7 multiply_multiply_fusion.1
  46.7 0.0 all-reduce.3.cloned.1.call-update
  46.7 31.8 %all-reduce.3.cloned.1.call-done = (f32[8192]{0:T(1024)}, f32[8192]{0:T(1024)}) async-done(((f32[8192]{0:T(1024)}, f32[8192]{0:T(1024)}), (f32[8192]{0:T(1024)}, f32[8192]{0:T(1024)})) %all-reduce.3.cloned.1.call-update) | async-done | bytes 65552 | tf_op jit(solution)/shard_map/psum | solution.py:75
  78.5 0.0 copy-done
  78.5 0.0 copy-done.1
  78.5 1.4 %divide_subtract_fusion = f32[8192]{0:T(1024)} fusion(f32[8192]{0:T(1024)S(1)} %copy-done, f32[8192]{0:T(1024)} %get-tuple-element.2, f32[8192]{0:T(1024)} %get-tuple-element.3, f32[8192]{0:T(1024)S(1)} %copy-done.1), kind=kLoop, calls=%fused_computation.14 | loop fusion | flops 24576 | bytes 163840 | tf_op jit(solution)/shard_map/sub | solution.py:77
  (4 shorter events, 0.1 us)
Async XLA Ops:
  7.2 71.3 %copy-start = (f32[8192]{0:T(1024)S(1)}, f32[8192]{0:T(1024)}, u32[]{:S(2)}) copy-start(f32[8192]{0:T(1024)} %param.13) | copy-start | bytes 98308
  7.2 71.3 %copy-start.1 = (f32[8192]{0:T(1024)S(1)}, f32[8192]{0:T(1024)}, u32[]{:S(2)}) copy-start(f32[8192]{0:T(1024)} %param.17) | copy-start | bytes 98308
  7.2 71.3 %all-reduce.3.cloned.1.call-start = ((), (), s32[]{:S(2)}) async-start(), calls=%async_computation | async-start | bytes 131072 | tf_op jit(solution)/shard_map/psum | solution.py:75
  7.2 18.4 %collective-permute-start = (bf16[1,1,8192]{2,1,0:T(2,128)(2,1)}, bf16[1,1,8192]{2,1,0:T(2,128)(2,1)S(1)}, u32[]{:S(2)}, u32[]{:S(2)}) collective-permute-start(bf16[1,1,8192]{2,1,0:T(2,128)(2,1)} %bitcast.48), channel_id=1, source_target_pairs={{0,1},{1,0},{2,3},{3,2},{4,5},{5,4},{6,7},{7,6},{8,9},{9,8},{10,11... | collective-permute-start | bytes 49160 | tf_op jit(solution)/shard_map/ppermute | solution.py:18
  29.0 4.0 %collective-permute-start.1 = (bf16[2,1,8192]{2,0,1:T(2,128)(2,1)S(1)}, bf16[2,1,8192]{2,0,1:T(2,128)(2,1)S(1)}, u32[]{:S(2)}, u32[]{:S(2)}) collective-permute-start(bf16[2,1,8192]{2,0,1:T(2,128)(2,1)S(1)} %get-tuple-element.9), channel_id=1, source_target_pairs={{0,2},{1,3},{2,0},{3,1},{4,6},{5,7},{6,4},{7,5},{8,10},{9,11},{10,... | collective-permute-start | bytes 98312 | tf_op jit(solution)/shard_map/ppermute | solution.py:18
  33.1 5.2 %collective-permute-start.2 = (bf16[4,1,8192]{2,0,1:T(4,128)(2,1)S(1)}, bf16[4,1,8192]{2,0,1:T(4,128)(2,1)S(1)}, u32[]{:S(2)}, u32[]{:S(2)}) collective-permute-start(bf16[4,1,8192]{2,0,1:T(4,128)(2,1)S(1)} %reshape.88), channel_id=1, source_target_pairs={{0,4},{1,5},{2,6},{3,7},{4,0},{5,1},{6,2},{7,3},{8,12},{9,13},{10,... | collective-permute-start | bytes 196616 | tf_op jit(solution)/shard_map/ppermute | solution.py:18
Sparse Core Ops, SparseCore 0:
  46.8 31.6 all-reduce.2
